TPU v7x, 128 devices: a whole 4x4x4 slice. The times are simulated.
128 devices in a mesh: expert: 8 (over x, core), shard: 16 (over z, y).
Axes of the slice: x: 4, y: 4, z: 4, core: 2. Of those that a mesh axis runs over, the one named last changes fastest.
Arguments:
- tokens_in: bfloat16 [4096, 4096], P(('expert', 'shard')), may hold values from -6 to 6
- out_grad: bfloat16 [4096, 2, 8192], P(('expert', 'shard')), may hold values from -6 to 6
- expert_ids: int32 [4096, 2], P(('expert', 'shard')), may hold values from 0 to 7, all different within a row; in each aligned block of 32 rows (0 to 31, 32 to 63, ...) at most 10 rows name the same one
- d_levels: int32 [8, 16], P('expert'), may hold values from 0 to 7
- f_levels: int32 [8, 32], P('expert', 'shard'), may hold values from 0 to 7
Outputs:
- ascent: bfloat16 [8, 4096, 8192], P('expert', None, 'shard')
Inputs may be any that keep to these rules, and one draw needn't show every extreme that they name: `expert_ids`: each token names two different experts; among the 64 entries of one device no expert is named more than 10 times, and 10 is reached on some device; every expert is named somewhere.
All inputs are finite; a program needn't handle non-finite values.
Results may differ from a plain program's by a relative error of at most 0.001.
Values may be sent and summed in bfloat16 or wider, within the bound.
No kernel may reach another device: no remote copies, remote signals or barrier semaphores. Data moves between devices by JAX's collectives and lax.ppermute only.
A program may use at most 128 MiB of HBM per device.

v0:
```python
import functools

import jax
import jax.numpy as jnp
from jax import lax
from jax.experimental import pallas as pl
from jax.experimental.pallas import tpu as pltpu
from jax.sharding import PartitionSpec as P

BLK = 256
BASE = 32
PANEL = 8
F32 = jnp.float32
BF = jnp.bfloat16
TN = (((0,), (0,)), ((), ()))


def iota(shape, dim):
    return lax.broadcasted_iota(jnp.int32, shape, dim)


def div(value, by):
    return (value * (65536 // by + 1)) >> 16


def onehot(hit):
    return jnp.where(hit, 1.0, 0.0).astype(BF)


def split2(x):
    high = x.astype(BF)
    return high, (x - high.astype(F32)).astype(BF)


def split3(x):
    high = x.astype(BF)
    rest = x - high.astype(F32)
    mid = rest.astype(BF)
    return high, mid, (rest - mid.astype(F32)).astype(BF)


def tn_full(a, b):
    ah, am, al = split3(a)
    bh, bm, bl = split3(b)
    return lax.dot_general(
        jnp.concatenate([ah, ah, am, ah, al, am], 0),
        jnp.concatenate([bh, bm, bh, bl, bh, bm], 0),
        TN,
        preferred_element_type=F32,
    )


def dot3(a, b):
    ah, al = a
    bh, bl = b
    return jnp.dot(
        jnp.concatenate([ah, ah, al], 1),
        jnp.concatenate([bh, bl, bh], 0),
        preferred_element_type=F32,
    )


def invert_base(packs):
    lane, sub = iota((BASE, 128), 1), iota((BASE, 128), 0)
    start = (lane // BASE) * BASE
    inner = lane - start
    packs = list(packs)
    for k0 in range(0, BASE, PANEL):
        cols = [
            [jnp.take_along_axis(x, start + (k0 + j), axis=1) for j in range(PANEL)] for x in packs
        ]
        for j in range(PANEL):
            k = k0 + j
            is_col, is_row = inner == k, sub == k
            for g, x in enumerate(packs):
                col = cols[g][j]
                inv = 1.0 / col[k : k + 1, :]
                row = jnp.where(is_col[:1], 1.0, x[k : k + 1, :]) * inv
                for jj in range(j + 1, PANEL):
                    other = cols[g][jj]
                    scaled = other[k : k + 1, :] * inv
                    cols[g][jj] = jnp.where(is_row, scaled, other - col * scaled)
                packs[g] = jnp.where(is_row, row, jnp.where(is_col, 0.0, x) - col * row)
    return packs


def invert_all(m_ref, count):
    per = 128 // BASE
    lane, sub = iota((BASE, BLK), 1), iota((BASE, BLK), 0)
    wide = iota((BLK, BLK), 1)
    for low in range(0, BLK, BASE):
        end = low + BASE
        packs = [
            jnp.concatenate(
                [m_ref[min(g + j, count - 1), low:end, low:end] for j in range(per)], axis=1
            )
            for g in range(0, count, per)
        ]
        packs = invert_base(packs)
        own = (lane >= low) & (lane < end)
        minus_eye = jnp.where(lane - low == sub, -1.0, 0.0)
        for m in range(count):
            at = (m % per) * BASE
            pivot = packs[m // per][:, at : at + BASE]
            rows = m_ref[m, low:end, :]
            new_rows = tn_full(pivot, jnp.where(own, minus_eye, rows))
            change = tn_full(jnp.where(own, 0.0, rows), new_rows)
            m_ref[m] = jnp.where((wide >= low) & (wide < end), 0.0, m_ref[m]) - change
            m_ref[m, low:end, :] = new_rows


def slots(id_col, id_row, first, step, capacity):
    shape = (id_col.shape[0], id_row.shape[1])
    earlier = iota(shape, 0) < first + step * iota(shape, 1)
    same = (id_col == id_row) & earlier
    rank = jnp.sum(jnp.where(same, 1, 0), axis=0, keepdims=True)
    return id_row, rank


def send_x_kernel(cap, parts, me_ref, col_ref, first_ref, second_ref, x_ref, *out_refs):
    groups, per = len(out_refs), out_refs[0].shape[0]
    rows, toks = groups * per, x_ref.shape[0]
    width = x_ref.shape[1] // parts
    hot = []
    for part in range(parts):
        total = None
        for j, ids in enumerate((first_ref, second_ref)):
            expert, rank = slots(col_ref[...], ids[...], j, 2, cap)
            ahead = expert - me_ref[0]
            ahead = jnp.where(ahead < 0, ahead + groups, ahead)
            hit = iota((rows, toks), 0) == ahead * per + part * cap + rank
            hit = jnp.where(hit, 1.0, 0.0)
            total = hit if total is None else total + hit
        hot.append(total.astype(BF))
    data = jnp.concatenate([x_ref[:, p * width : (p + 1) * width] for p in range(parts)], 0)
    out = jnp.dot(jnp.concatenate(hot, 1), data, preferred_element_type=F32)
    for k, ref in enumerate(out_refs):
        ref[...] = out[k * per : (k + 1) * per].astype(BF)


def take_x_kernel(cap, parts, me_ref, *refs):
    *in_refs, out_ref = refs
    groups, (per, width) = len(in_refs), in_refs[0].shape
    data = jnp.concatenate([ref[...] for ref in in_refs], 0)
    shape = (groups * cap, groups * per)
    row = iota(shape, 0)
    source = div(row, cap)
    behind = me_ref[0] - source
    behind = jnp.where(behind < 0, behind + groups, behind)
    base = behind * per + (row - source * cap)
    for part in range(parts):
        pick = onehot(iota(shape, 1) == base + part * cap)
        got = jnp.dot(pick, data, preferred_element_type=F32)
        out_ref[:, part * width : (part + 1) * width] = got.astype(BF)


def payload_kernel(cap, rows, ng, col_ref, row_ref, g_ref, out_ref, hot_ref, add_ref):
    pair, groups = out_ref.shape[:2]
    pairs = g_ref.shape[0]
    total = groups * rows

    @pl.when(pl.program_id(0) == 0)
    def _():
        expert, rank = slots(col_ref[...], row_ref[...], 0, 1, cap)
        row = iota((total, pairs), 0)
        for part in range(ng):
            target = expert * rows + part * cap + rank
            hot_ref[:, part * pairs : (part + 1) * pairs] = onehot(row == target)
        marked = row == row_ref[...] * rows + ng * cap
        add_ref[...] = jnp.sum(jnp.where(marked, 1.0, 0.0), axis=1, keepdims=True)

    data = jnp.concatenate(
        [
            jnp.concatenate(
                [g_ref[:, (t * ng + p) * 128 : (t * ng + p + 1) * 128] for t in range(pair)], 1
            )
            for p in range(ng)
        ],
        0,
    )
    out = jnp.dot(hot_ref[...], data, preferred_element_type=F32) + add_ref[...]
    for t in range(pair):
        piece = out[:, t * 128 : (t + 1) * 128].astype(BF)
        out_ref[t] = piece.reshape(groups, rows, 128)


def set_block(m_ref, at, cov, count, level):
    eye = iota((BLK, BLK), 0) == iota((BLK, BLK), 1)
    damp = 0.05 * jnp.exp(0.4 * jnp.full((1, 1), level, F32))
    m_ref[at] = cov * (1.0 / count) + jnp.where(eye, damp, 0.0)


def hidden_kernel(cap, ng, lev_ref, in_ref, h_ref, s_ref, count_ref, m_ref):
    groups, shards, rows, _ = in_ref.shape
    live = groups * cap
    shape = (live, groups * rows)
    row = iota(shape, 0)
    source = div(row, cap)
    base = source * rows + (row - source * cap)
    pick = jnp.concatenate([onehot(iota(shape, 1) == base + p * cap) for p in range(ng)], 0)
    total = jnp.zeros((1, 128), F32)
    for s in range(shards):
        data = in_ref[:, s].reshape(groups * rows, 128)
        got = jnp.dot(pick, data, preferred_element_type=F32).astype(BF)
        for p in range(ng):
            h_ref[s * live : (s + 1) * live, p * 128 : (p + 1) * 128] = got[
                p * live : (p + 1) * live
            ]
        for g in range(groups):
            total = total + in_ref[g, s, ng * cap : ng * cap + 1, :].astype(F32)
    count_ref[...] = total
    for c in range(m_ref.shape[0]):
        part = h_ref[:, c * BLK : (c + 1) * BLK]
        cov = lax.dot_general(part, part, TN, preferred_element_type=F32)
        set_block(m_ref, c, cov, total[:, :1], lev_ref[c])
    invert_all(m_ref, m_ref.shape[0])
    s_ref[...] = -m_ref[...]


def solve_kernel(lev_ref, count_ref, x_hbm, h_ref, s_ref, out_hbm, sum_ref, x_ref, m_ref, g_ref,
                 x_sem, out_sem):
    blocks, _, width = g_ref.shape
    cuts = [slice(c * BLK, (c + 1) * BLK) for c in range(width // BLK)]

    def fetch(b):
        columns = pl.ds(b * BLK, BLK)
        return pltpu.make_async_copy(x_hbm.at[:, columns], x_ref.at[b], x_sem.at[b])

    def store(b):
        return pltpu.make_async_copy(g_ref.at[b], out_hbm.at[b], out_sem.at[b])

    for b in range(blocks):
        fetch(b).start()
    for b in range(blocks):
        fetch(b).wait()
        x = x_ref[b]
        both = lax.dot_general(
            x, jnp.concatenate([x, h_ref[...]], 1), TN, preferred_element_type=F32
        )
        set_block(m_ref, b, both[:, :BLK], count_ref[:, :1], lev_ref[b])
        g_ref[b] = both[:, BLK:]
    invert_all(m_ref, blocks)
    right = [split2(s_ref[c]) for c in range(len(cuts))]
    total = jnp.zeros((8, 128), F32)
    for b in range(blocks):
        left = split2(-m_ref[b])
        for c, cut in enumerate(cuts):
            out = dot3(left, split2(dot3(split2(g_ref[b, :, cut]), right[c])))
            g_ref[b, :, cut] = out
            square = (out * out).reshape(BLK // 8, 8, BLK).sum(axis=0)
            for k in range(BLK // 128):
                total = total + square[:, k * 128 : (k + 1) * 128]
        store(b).start()
    sum_ref[...] = total
    for b in range(blocks):
        store(b).wait()


def scale_kernel(count, norm_ref, in_ref, out_ref):
    total = jnp.sum(jnp.sum(norm_ref[...], axis=0, keepdims=True), axis=1, keepdims=True)
    out_ref[...] = (in_ref[...] * lax.rsqrt(total / count + 1e-06)).astype(BF)


def in_hbm(*arrays):
    return [pltpu.with_memory_space_constraint(array, pltpu.HBM) for array in arrays]


def full(shape):
    return pl.BlockSpec(shape, lambda *_: (0,) * len(shape))


def local(tokens_in, out_grad, expert_ids, d_levels, f_levels):
    groups, shards = lax.axis_size("expert"), lax.axis_size("shard")
    toks, width = tokens_in.shape
    ff = out_grad.shape[2]
    ff_dev = ff // shards
    cap = min(toks, max(2, 5 * toks // (2 * groups)))
    live = groups * cap
    parts = 4
    ng = ff_dev // 128
    rows = -(-(ng * cap + 1) // 16) * 16
    vm, sm = pl.BlockSpec(memory_space=pltpu.VMEM), pl.BlockSpec(memory_space=pltpu.SMEM)

    def call(kernel, mib=16, **kwargs):
        params = pltpu.CompilerParams(vmem_limit_bytes=mib << 20)
        return pl.pallas_call(kernel, compiler_params=params, **kwargs)

    id_row = expert_ids.reshape(1, 2 * toks)
    id_col = expert_ids.reshape(2 * toks, 1)
    first, second = expert_ids[:, 0].reshape(1, toks), expert_ids[:, 1].reshape(1, toks)

    me = lax.axis_index("expert").astype(jnp.int32).reshape(1)
    per = cap * parts
    x_send = call(
        functools.partial(send_x_kernel, cap, parts),
        out_shape=[jax.ShapeDtypeStruct((per, width // parts), BF)] * groups,
        in_specs=[sm] + [vm] * 4,
        name="send_x",
    )(me, id_col, first, second, tokens_in)
    x_recv = [x_send[0]] + [
        lax.ppermute(x_send[k], "expert", [(e, (e + k) % groups) for e in range(groups)])
        for k in range(1, groups)
    ]
    payload = call(
        functools.partial(payload_kernel, cap, rows, ng),
        out_shape=jax.ShapeDtypeStruct((shards, groups, rows, 128), BF),
        grid=(shards // 2,),
        in_specs=[
            full((2 * toks, 1)),
            full((1, 2 * toks)),
            pl.BlockSpec((2 * toks, 2 * ff_dev), lambda s: (0, s)),
        ],
        out_specs=pl.BlockSpec((2, groups, rows, 128), lambda s: (s, 0, 0, 0)),
        scratch_shapes=[
            pltpu.VMEM((groups * rows, ng * 2 * toks), BF),
            pltpu.VMEM((groups * rows, 1), F32),
        ],
        name="payload",
    )(id_col, id_row, out_grad.reshape(2 * toks, ff))
    received = lax.all_to_all(payload, "shard", 0, 0, tiled=True)
    received, *x_recv = lax.optimization_barrier((received, *x_recv))
    x_group = call(
        functools.partial(take_x_kernel, cap, parts),
        out_shape=jax.ShapeDtypeStruct((live, width), BF),
        in_specs=[sm] + [vm] * groups,
        name="take_x",
    )(me, *x_recv)
    rows_x = lax.all_gather(x_group, "shard", axis=0, tiled=True)

    received = lax.all_to_all(received.transpose(1, 0, 2, 3), "expert", 0, 0, tiled=True)

    hidden = ff_dev // BLK
    rows_g, inv_f, count = call(
        functools.partial(hidden_kernel, cap, ng),
        out_shape=[
            jax.ShapeDtypeStruct((shards * live, ff_dev), BF),
            jax.ShapeDtypeStruct((hidden, BLK, BLK), F32),
            jax.ShapeDtypeStruct((1, 128), F32),
        ],
        in_specs=[sm, vm],
        out_specs=(vm,) * 3,
        scratch_shapes=[pltpu.VMEM((hidden, BLK, BLK), F32)],
        name="hidden",
    )(f_levels[0].astype(F32), received)

    blocks = width // BLK
    hbm = pl.BlockSpec(memory_space=pltpu.HBM)
    precond, square = call(
        solve_kernel,
        mib=44,
        out_shape=(
            pltpu.HBM((blocks, BLK, ff_dev), F32),
            jax.ShapeDtypeStruct((8, 128), F32),
        ),
        in_specs=[sm, vm, hbm, vm, vm],
        out_specs=(hbm, vm),
        scratch_shapes=[
            pltpu.VMEM((blocks, shards * live, BLK), BF),
            pltpu.VMEM((blocks, BLK, BLK), F32),
            pltpu.VMEM((blocks, BLK, ff_dev), F32),
            pltpu.SemaphoreType.DMA((blocks,)),
            pltpu.SemaphoreType.DMA((blocks,)),
        ],
        name="solve",
    )(d_levels[0].astype(F32), count, rows_x, rows_g, inv_f)

    devices = groups * shards
    norm = jnp.sum(square, axis=0, keepdims=True)
    norm = lax.all_to_all(
        jnp.broadcast_to(norm, (devices, 128)), ("expert", "shard"), 0, 0, tiled=True
    )
    tile = width // 4
    ascent = call(
        functools.partial(scale_kernel, float(groups * width * ff)),
        out_shape=jax.ShapeDtypeStruct((width, ff_dev), BF),
        grid=(4,),
        in_specs=[full((devices, 128)), pl.BlockSpec((tile, ff_dev), lambda i: (i, 0))],
        out_specs=pl.BlockSpec((tile, ff_dev), lambda i: (i, 0)),
        name="scale",
    )(norm, *in_hbm(precond.reshape(width, ff_dev)))
    return ascent[None]


def solution(mesh):
    return jax.shard_map(
        local,
        mesh=mesh,
        in_specs=(
            P(("expert", "shard"), None),
            P(("expert", "shard"), None, None),
            P(("expert", "shard"), None),
            P("expert", None),
            P("expert", "shard"),
        ),
        out_specs=P("expert", None, "shard"),
        check_vma=False,
    )
```

profile of v0, /device:TPU:1, one launch (start us, length us, event | category | flops | bytes accessed | tf_op | source)
XLA Modules:
  0.0 219.5 jit_solution(14516776917503604952)
XLA Ops:
  6.5 0.8 copy.16
  7.3 0.1 reshape.24.row_ref
  7.4 0.1 reshape.28.col_ref
  7.5 1.5 reshape.25.g_ref
  8.9 4.2 %payload.1 = bf16[16,8,48,128]{3,2,1,0:T(8,128)(2,1)} custom-call(s32[64,1]{1,0:T(8,128)S(1)} %reshape.28.col_ref, s32[1,64]{1,0:T(1,128)S(1)} %reshape.24.row_ref, bf16[64,8192]{1,0:T(8,128)(2,1)S(1)} %reshape.25.g_ref), custom_call_target="tpu_custom_call" | custom-call | tf_op jit(solution)/shard_map/payload/pallas_call | solution.py:304
  13.2 8.7 %all-to-all-start = ((bf16[16,8,48,128]{3,2,1,0:T(8,128)(2,1)}), bf16[16,8,48,128]{3,2,1,0:T(8,128)(2,1)S(1)}, u32[]{:S(2)}, u32[]{:S(2)}) async-start(bf16[16,8,48,128]{3,2,1,0:T(8,128)(2,1)} %payload.1), calls=%async_computation | async-start | bytes 3145728 | tf_op jit(solution)/shard_map/all_to_all | solution.py:320
  21.9 0.0 all-gather.2.cloned.1.call-start
  22.0 0.5 send_x.1
  22.5 2.1 collective-permute-start
  24.6 1.2 collective-permute-start.1
  25.8 1.6 collective-permute-start.2
  27.4 0.5 collective-permute-start.3
  27.9 1.9 collective-permute-start.4
  29.8 0.0 collective-permute-done.refs_1_
  29.8 0.7 collective-permute-start.5
  30.5 0.0 collective-permute-done.1.refs_2_
  30.5 1.7 collective-permute-start.6
  32.2 0.0 collective-permute-done.2.refs_3_
  32.2 2.5 %collective-permute-done.3.refs_4_ = bf16[40,1024]{1,0:T(8,128)(2,1)S(1)} collective-permute-done((bf16[40,1024]{1,0:T(8,128)(2,1)S(1)}, bf16[40,1024]{1,0:T(8,128)(2,1)S(1)}, u32[]{:S(2)}, u32[]{:S(2)}) %collective-permute-start.3) | collective-permute-done | bytes 81952 | tf_op jit(solution)/shard_map/ppermute | solution.py:301
  34.7 0.6 collective-permute-done.4.refs_5_
  35.3 1.2 collective-permute-done.6.refs_7_
  36.5 8.3 %all-to-all-done = bf16[16,8,48,128]{3,2,1,0:T(8,128)(2,1)S(1)} async-done(((bf16[16,8,48,128]{3,2,1,0:T(8,128)(2,1)}), bf16[16,8,48,128]{3,2,1,0:T(8,128)(2,1)S(1)}, u32[]{:S(2)}, u32[]{:S(2)}) %all-to-all-start) | async-done | bytes 1572896 | tf_op jit(solution)/shard_map/all_to_all | solution.py:320
  44.8 1.5 take_x.1
  46.3 0.0 all-gather.2.cloned.1.call-update
  46.3 1.2 copy.22
  47.6 7.5 %all-to-all-start.1 = ((bf16[8,16,48,128]{3,2,1,0:T(8,128)(2,1)}), bf16[8,16,48,128]{3,2,1,0:T(8,128)(2,1)S(1)}, u32[]{:S(2)}, u32[]{:S(2)}) async-start(bf16[8,16,48,128]{3,2,1,0:T(8,128)(2,1)} %bitcast.17), calls=%async_computation.1 | async-start | bytes 3145728 | tf_op jit(solution)/shard_map/all_to_all | solution.py:330
  55.1 20.2 %all-to-all-done.1.in_ref = bf16[8,16,48,128]{3,2,1,0:T(8,128)(2,1)S(1)} async-done(((bf16[8,16,48,128]{3,2,1,0:T(8,128)(2,1)}), bf16[8,16,48,128]{3,2,1,0:T(8,128)(2,1)S(1)}, u32[]{:S(2)}, u32[]{:S(2)}) %all-to-all-start.1) | async-done | bytes 1572896 | tf_op jit(solution)/shard_map/all_to_all | solution.py:330
  75.3 13.4 %hidden.1 = (bf16[1280,512]{1,0:T(8,128)(2,1)S(1)}, f32[2,256,256]{2,1,0:T(8,128)S(1)}, f32[1,128]{1,0:T(1,128)S(1)}) custom-call(f32[2]{0:T(128)S(1)} %convert_bitcast_fusion.lev_ref, bf16[8,16,48,128]{3,2,1,0:T(8,128)(2,1)S(1)} %all-to-all-done.1.in_ref), custom_call_target="tpu_custom_call" | custom-call | tf_op jit(solution)/shard_map/hidden/pallas_call | solution.py:333
  88.7 37.3 %all-gather.2.cloned.1.call-done.x_hbm = bf16[1280,4096]{1,0:T(8,128)(2,1)} async-done(((bf16[80,4096]{1,0:T(8,128)(2,1)}), bf16[1280,4096]{1,0:T(8,128)(2,1)}) %all-gather.2.cloned.1.call-update) | async-done | bytes 10485776 | tf_op jit(solution)/shard_map/all_gather | solution.py:328
  126.0 62.6 %solve.1 = (f32[16,256,512]{2,1,0:T(8,128)}, f32[8,128]{1,0:T(8,128)S(1)}) custom-call(f32[16]{0:T(128)S(1)} %convert_bitcast_fusion.1.lev_ref, f32[1,128]{1,0:T(1,128)S(1)} %get-tuple-element.36.count_ref, bf16[1280,4096]{1,0:T(8,128)(2,1)} %all-gather.2.cloned.1.call-done.x_hbm, bf16[1280,512]{1,0:T(8,128)(2,1)S(1)} %get-tuple-element.45.h_ref, ...), custom_call_target="tpu_custom_call" | custom-call | tf_op jit(solution)/shard_map/solve/pallas_call | solution.py:348
  188.7 17.5 %all_to_all.18 = f32[128,1,128]{2,1,0:T(1,128)S(1)} all-to-all(f32[128,1,128]{2,1,0:T(1,128)S(1)} %broadcast_in_dim.4), channel_id=1, replica_groups=mesh['expert'=8,'shard'=16] {'expert','shard'}, dimensions={0} | all-to-all | bytes 131072 | tf_op jit(solution)/shard_map/all_to_all | solution.py:369
  206.3 6.2 %scale.1 = bf16[4096,512]{1,0:T(8,128)(2,1)} custom-call(f32[128,128]{1,0:T(8,128)S(1)} %bitcast.15, f32[4096,512]{1,0:T(8,128)} %bitcast.16), custom_call_target="tpu_custom_call" | custom-call | tf_op jit(solution)/shard_map/scale/pallas_call | solution.py:373
  (14 shorter events, 0.1 us)
Async XLA Ops:
  13.2 8.8 %copy-start.1 = (s32[32,2]{0,1:T(2,128)S(1)}, s32[32,2]{0,1:T(2,128)}, u32[]{:S(2)}) copy-start(s32[32,2]{0,1:T(2,128)} %param.7) | copy-start | bytes 772
  13.2 8.8 %copy-start = (bf16[32,4096]{1,0:T(8,128)(2,1)S(1)}, bf16[32,4096]{1,0:T(8,128)(2,1)}, u32[]{:S(2)}) copy-start(bf16[32,4096]{1,0:T(8,128)(2,1)} %x_ref.1) | copy-start | bytes 786436
  13.2 31.6 %all-to-all-start = ((bf16[16,8,48,128]{3,2,1,0:T(8,128)(2,1)}), bf16[16,8,48,128]{3,2,1,0:T(8,128)(2,1)S(1)}, u32[]{:S(2)}, u32[]{:S(2)}) async-start(bf16[16,8,48,128]{3,2,1,0:T(8,128)(2,1)} %payload.1), calls=%async_computation | async-start | bytes 3145728 | tf_op jit(solution)/shard_map/all_to_all | solution.py:320
  21.9 104.1 %all-gather.2.cloned.1.call-start = ((), (), s32[]{:S(2)}) async-start(), calls=%async_computation.3 | async-start | bytes 11141120 | tf_op jit(solution)/shard_map/all_gather | solution.py:328
  22.5 7.4 %collective-permute-start = (bf16[40,1024]{1,0:T(8,128)(2,1)S(1)}, bf16[40,1024]{1,0:T(8,128)(2,1)S(1)}, u32[]{:S(2)}, u32[]{:S(2)}) collective-permute-start(bf16[40,1024]{1,0:T(8,128)(2,1)S(1)} %get-tuple-element.28), channel_id=1, source_target_pairs={{0,16},{16,32},{32,48},{48,64},{64,80},{80,96},{96,112},{112,0},{1... | collective-permute-start | bytes 245768 | tf_op jit(solution)/shard_map/ppermute | solution.py:301
  24.6 5.9 %collective-permute-start.1 = (bf16[40,1024]{1,0:T(8,128)(2,1)S(1)}, bf16[40,1024]{1,0:T(8,128)(2,1)S(1)}, u32[]{:S(2)}, u32[]{:S(2)}) collective-permute-start(bf16[40,1024]{1,0:T(8,128)(2,1)S(1)} %get-tuple-element.29), channel_id=1, source_target_pairs={{0,32},{16,48},{32,64},{48,80},{64,96},{80,112},{96,0},{112,16},{1... | collective-permute-start | bytes 245768 | tf_op jit(solution)/shard_map/ppermute | solution.py:301
  25.8 6.4 %collective-permute-start.2 = (bf16[40,1024]{1,0:T(8,128)(2,1)S(1)}, bf16[40,1024]{1,0:T(8,128)(2,1)S(1)}, u32[]{:S(2)}, u32[]{:S(2)}) collective-permute-start(bf16[40,1024]{1,0:T(8,128)(2,1)S(1)} %get-tuple-element.30), channel_id=1, source_target_pairs={{0,48},{16,64},{32,80},{48,96},{64,112},{80,0},{96,16},{112,32},{1... | collective-permute-start | bytes 245768 | tf_op jit(solution)/shard_map/ppermute | solution.py:301
  27.4 7.3 %collective-permute-start.3 = (bf16[40,1024]{1,0:T(8,128)(2,1)S(1)}, bf16[40,1024]{1,0:T(8,128)(2,1)S(1)}, u32[]{:S(2)}, u32[]{:S(2)}) collective-permute-start(bf16[40,1024]{1,0:T(8,128)(2,1)S(1)} %get-tuple-element.31), channel_id=1, source_target_pairs={{0,64},{16,80},{32,96},{48,112},{64,0},{80,16},{96,32},{112,48},{1... | collective-permute-start | bytes 245768 | tf_op jit(solution)/shard_map/ppermute | solution.py:301
  27.9 7.4 %collective-permute-start.4 = (bf16[40,1024]{1,0:T(8,128)(2,1)S(1)}, bf16[40,1024]{1,0:T(8,128)(2,1)S(1)}, u32[]{:S(2)}, u32[]{:S(2)}) collective-permute-start(bf16[40,1024]{1,0:T(8,128)(2,1)S(1)} %get-tuple-element.32), channel_id=1, source_target_pairs={{0,80},{16,96},{32,112},{48,0},{64,16},{80,32},{96,48},{112,64},{1... | collective-permute-start | bytes 245768 | tf_op jit(solution)/shard_map/ppermute | solution.py:301
  29.8 5.4 %collective-permute-start.5 = (bf16[40,1024]{1,0:T(8,128)(2,1)S(1)}, bf16[40,1024]{1,0:T(8,128)(2,1)S(1)}, u32[]{:S(2)}, u32[]{:S(2)}) collective-permute-start(bf16[40,1024]{1,0:T(8,128)(2,1)S(1)} %get-tuple-element.33), channel_id=1, source_target_pairs={{0,96},{16,112},{32,0},{48,16},{64,32},{80,48},{96,64},{112,80},{1... | collective-permute-start | bytes 245768 | tf_op jit(solution)/shard_map/ppermute | solution.py:301
  30.5 6.0 %collective-permute-start.6 = (bf16[40,1024]{1,0:T(8,128)(2,1)S(1)}, bf16[40,1024]{1,0:T(8,128)(2,1)S(1)}, u32[]{:S(2)}, u32[]{:S(2)}) collective-permute-start(bf16[40,1024]{1,0:T(8,128)(2,1)S(1)} %get-tuple-element.34), channel_id=1, source_target_pairs={{0,112},{16,0},{32,16},{48,32},{64,48},{80,64},{96,80},{112,96},{1... | collective-permute-start | bytes 245768 | tf_op jit(solution)/shard_map/ppermute | solution.py:301
  47.6 7.5 %copy-start.2 = (s32[1,16]{1,0:T(1,128)S(1)}, s32[1,16]{1,0:T(1,128)}, u32[]{:S(2)}) copy-start(s32[1,16]{1,0:T(1,128)} %param.8) | copy-start | bytes 196
  47.6 7.5 %copy-start.3 = (s32[1,2]{1,0:T(1,128)S(1)}, s32[1,2]{1,0:T(1,128)}, u32[]{:S(2)}) copy-start(s32[1,2]{1,0:T(1,128)} %param.9) | copy-start | bytes 28
  47.6 27.7 %all-to-all-start.1 = ((bf16[8,16,48,128]{3,2,1,0:T(8,128)(2,1)}), bf16[8,16,48,128]{3,2,1,0:T(8,128)(2,1)S(1)}, u32[]{:S(2)}, u32[]{:S(2)}) async-start(bf16[8,16,48,128]{3,2,1,0:T(8,128)(2,1)} %bitcast.17), calls=%async_computation.1 | async-start | bytes 3145728 | tf_op jit(solution)/shard_map/all_to_all | solution.py:330
Sparse Core Ops, SparseCore 0:
  46.5 79.5 all-gather.1
where the time goes:
time: 223 us; the launch traced here: 220 us
  Pallas kernels  88.5 us (40%)
  waiting for transfers between devices  70.1 us (31%)
  starting transfers between devices  26 us (12%)
  blocking collectives  17.5 us (8%)
  between operations  13.7 us (6%)
  local copies, waits for them, and re-layouts  3.71 us (2%)
    pallas_call x1, Pallas kernels, local(): call(solve_kernel, mib=44, out_shape=(pltpu.HBM((blocks, BLK, ff_dev), F3...  62.6 us
    all_gather x1, waiting for transfers between devices, local(): rows_x = lax.all_gather(x_group, 'shard', axis=0, tiled=True)  37.3 us
    all_to_all x1, waiting for transfers between devices, local(): lax.all_to_all(received.transpose(1, 0, 2, 3), 'expert', 0, 0, tiled=True)  20.2 us
    all_to_all x1, blocking collectives, local(): lax.all_to_all(jnp.broadcast_to(norm, (devices, 128)), ('expert', 'shard'...  17.5 us
    pallas_call x1, Pallas kernels, local(): call(functools.partial(hidden_kernel, cap, ng), out_shape=[jax.ShapeDtype...  13.4 us
    ppermute x7, starting transfers between devices, local(): lax.ppermute(x_send[k], 'expert', [(e, (e + k) % groups) for e in range(g...  9.68 us
    all_to_all x1, starting transfers between devices, local(): received = lax.all_to_all(payload, 'shard', 0, 0, tiled=True)  8.73 us
    all_to_all x1, waiting for transfers between devices, local(): received = lax.all_to_all(payload, 'shard', 0, 0, tiled=True)  8.27 us
  transfers between devices with their start and end apart: 10, of which 6 were waited for; matrix products, arithmetic and copies ran while one was open for 1% of the time, Pallas kernels for 6%

commit v1 on v0

--- a/solution.py
+++ b/solution.py
@@ -217,23 +217,15 @@
     s_ref[...] = -m_ref[...]
 
 
-def solve_kernel(lev_ref, count_ref, x_hbm, h_ref, s_ref, out_hbm, sum_ref, x_ref, m_ref, g_ref,
-                 x_sem, out_sem):
+def solve_kernel(lev_ref, count_ref, x_ref, h_ref, s_ref, out_hbm, sum_ref, m_ref, g_ref, out_sem):
     blocks, _, width = g_ref.shape
     cuts = [slice(c * BLK, (c + 1) * BLK) for c in range(width // BLK)]
 
-    def fetch(b):
-        columns = pl.ds(b * BLK, BLK)
-        return pltpu.make_async_copy(x_hbm.at[:, columns], x_ref.at[b], x_sem.at[b])
-
     def store(b):
         return pltpu.make_async_copy(g_ref.at[b], out_hbm.at[b], out_sem.at[b])
 
     for b in range(blocks):
-        fetch(b).start()
-    for b in range(blocks):
-        fetch(b).wait()
-        x = x_ref[b]
+        x = x_ref[:, b * BLK : (b + 1) * BLK]
         both = lax.dot_general(
             x, jnp.concatenate([x, h_ref[...]], 1), TN, preferred_element_type=F32
         )
@@ -318,7 +310,6 @@
         name="payload",
     )(id_col, id_row, out_grad.reshape(2 * toks, ff))
     received = lax.all_to_all(payload, "shard", 0, 0, tiled=True)
-    received, *x_recv = lax.optimization_barrier((received, *x_recv))
     x_group = call(
         functools.partial(take_x_kernel, cap, parts),
         out_shape=jax.ShapeDtypeStruct((live, width), BF),
@@ -352,13 +343,11 @@
             pltpu.HBM((blocks, BLK, ff_dev), F32),
             jax.ShapeDtypeStruct((8, 128), F32),
         ),
-        in_specs=[sm, vm, hbm, vm, vm],
+        in_specs=[sm, vm, vm, vm, vm],
         out_specs=(hbm, vm),
         scratch_shapes=[
-            pltpu.VMEM((blocks, shards * live, BLK), BF),
             pltpu.VMEM((blocks, BLK, BLK), F32),
             pltpu.VMEM((blocks, BLK, ff_dev), F32),
-            pltpu.SemaphoreType.DMA((blocks,)),
             pltpu.SemaphoreType.DMA((blocks,)),
         ],
         name="solve",

time: 223 us -> 199 us (0.89)
  blocking collectives: 17.5 us -> 58.1 us
  waiting for transfers between devices: 70.1 us -> 35.6 us
  Pallas kernels: 88.5 us -> 67.4 us
  starting transfers between devices: 26 us -> 15.6 us
    all_to_all x0 -> x1, blocking collectives: none -> 40.7 us  [local(): received = lax.all_to_all(payload, 'shard', 0, 0, tiled=True)]
    all_gather x1, waiting for transfers between devices: 37.3 us -> 11.1 us  [local(): rows_x = lax.all_gather(x_group, 'shard', axis=0, tiled=True)]
    pallas_call x1, Pallas kernels: 62.6 us -> 43.5 us  [local(): call(solve_kernel, mib=44, out_shape=(pltpu.HBM((blocks, BLK, ff_dev), F3...]
    all_to_all x1 -> x0, starting transfers between devices: 8.73 us -> none  [local(): received = lax.all_to_all(payload, 'shard', 0, 0, tiled=True)]
    all_to_all x1 -> x0, waiting for transfers between devices: 8.27 us -> none  [local(): received = lax.all_to_all(payload, 'shard', 0, 0, tiled=True)]
  transfers between devices with their start and end apart: 10 -> 9, of which waited for: 6 -> 6; matrix products, arithmetic and copies ran while one was open for 1% -> 1% of each run, Pallas kernels for 6% -> 8%
where the time goes in v1:
time: 199 us; the launch traced here: 195 us
  Pallas kernels  67.4 us (34%)
  blocking collectives  58.1 us (29%)
  waiting for transfers between devices  35.6 us (18%)
  starting transfers between devices  15.6 us (8%)
  between operations  13.7 us (7%)
  local copies, waits for them, and re-layouts  4.38 us (2%)
    pallas_call x1, Pallas kernels, local(): call(solve_kernel, mib=44, out_shape=(pltpu.HBM((blocks, BLK, ff_dev), F3...  43.5 us
    all_to_all x1, blocking collectives, local(): received = lax.all_to_all(payload, 'shard', 0, 0, tiled=True)  40.7 us
    all_to_all x1, waiting for transfers between devices, local(): lax.all_to_all(received.transpose(1, 0, 2, 3), 'expert', 0, 0, tiled=True)  20.5 us
    all_to_all x1, blocking collectives, local(): lax.all_to_all(jnp.broadcast_to(norm, (devices, 128)), ('expert', 'shard'...  17.4 us
    pallas_call x1, Pallas kernels, local(): call(functools.partial(hidden_kernel, cap, ng), out_shape=[jax.ShapeDtype...  13.4 us
    all_gather x1, waiting for transfers between devices, local(): rows_x = lax.all_gather(x_group, 'shard', axis=0, tiled=True)  11.1 us
    ppermute x7, starting transfers between devices, local(): lax.ppermute(x_send[k], 'expert', [(e, (e + k) % groups) for e in range(g...  10.2 us
    pallas_call x1, Pallas kernels, local(): call(functools.partial(scale_kernel, float(groups * width * ff)), out_sha...  6.24 us
  transfers between devices with their start and end apart: 9, of which 6 were waited for; matrix products, arithmetic and copies ran while one was open for 1% of the time, Pallas kernels for 8%

profile of v1, /device:TPU:1, one launch (start us, length us, event | category | flops | bytes accessed | tf_op | source)
XLA Modules:
  0.0 194.9 jit_solution(8251632107149515409)
XLA Ops:
  6.5 0.8 slice_bitcast_fusion
  7.3 0.8 copy.16
  8.1 0.1 reshape.28.col_ref
  8.1 0.9 copy-done
  9.1 0.5 send_x.1
  9.6 2.6 %collective-permute-start = (bf16[40,1024]{1,0:T(8,128)(2,1)S(1)}, bf16[40,1024]{1,0:T(8,128)(2,1)S(1)}, u32[]{:S(2)}, u32[]{:S(2)}) collective-permute-start(bf16[40,1024]{1,0:T(8,128)(2,1)S(1)} %get-tuple-element.20), channel_id=1, source_target_pairs={{0,16},{16,32},{32,48},{48,64},{64,80},{80,96},{96,112},{112,0},{1... | collective-permute-start | bytes 245768 | tf_op jit(solution)/shard_map/ppermute | solution.py:293
  12.2 1.2 collective-permute-start.1
  13.4 1.6 collective-permute-start.2
  15.0 0.5 collective-permute-start.3
  15.5 1.9 collective-permute-start.4
  17.4 0.0 collective-permute-done.refs_1_
  17.4 0.7 collective-permute-start.5
  18.1 1.7 collective-permute-start.6
  19.8 0.0 collective-permute-done.2.refs_3_
  19.8 2.2 %collective-permute-done.3.refs_4_ = bf16[40,1024]{1,0:T(8,128)(2,1)S(1)} collective-permute-done((bf16[40,1024]{1,0:T(8,128)(2,1)S(1)}, bf16[40,1024]{1,0:T(8,128)(2,1)S(1)}, u32[]{:S(2)}, u32[]{:S(2)}) %collective-permute-start.3) | collective-permute-done | bytes 81952 | tf_op jit(solution)/shard_map/ppermute | solution.py:293
  22.0 0.6 collective-permute-done.4.refs_5_
  22.6 0.2 collective-permute-done.5.refs_6_
  22.8 1.1 collective-permute-done.6.refs_7_
  23.8 1.5 take_x.1
  25.4 0.0 all-gather.2.cloned.1.call-update
  25.4 0.1 reshape.24.row_ref
  25.5 0.4 reshape.25.g_ref
  25.9 2.3 %payload.1 = bf16[16,8,48,128]{3,2,1,0:T(8,128)(2,1)S(1)} custom-call(s32[64,1]{1,0:T(8,128)S(1)} %reshape.28.col_ref, s32[1,64]{1,0:T(1,128)S(1)} %reshape.24.row_ref, bf16[64,8192]{1,0:T(8,128)(2,1)S(1)} %reshape.25.g_ref), custom_call_target="tpu_custom_call" | custom-call | tf_op jit(solution)/shard_map/payload/pallas_call | solution.py:296
  28.2 40.7 %all_to_all.18 = bf16[16,8,48,128]{3,2,1,0:T(8,128)(2,1)S(1)} all-to-all(bf16[16,8,48,128]{3,2,1,0:T(8,128)(2,1)S(1)} %payload.1), channel_id=1, replica_groups=mesh['expert'=8,'shard'=16] {'shard'}, dimensions={0} | all-to-all | bytes 3145728 | tf_op jit(solution)/shard_map/all_to_all | solution.py:312
  68.9 1.2 copy.22
  70.1 5.4 %all-to-all-start.1 = ((bf16[8,16,48,128]{3,2,1,0:T(8,128)(2,1)}), bf16[8,16,48,128]{3,2,1,0:T(8,128)(2,1)S(1)}, u32[]{:S(2)}, u32[]{:S(2)}) async-start(bf16[8,16,48,128]{3,2,1,0:T(8,128)(2,1)} %bitcast.14), calls=%async_computation.1 | async-start | bytes 3145728 | tf_op jit(solution)/shard_map/all_to_all | solution.py:321
  75.6 20.5 %all-to-all-done.1.in_ref = bf16[8,16,48,128]{3,2,1,0:T(8,128)(2,1)S(1)} async-done(((bf16[8,16,48,128]{3,2,1,0:T(8,128)(2,1)}), bf16[8,16,48,128]{3,2,1,0:T(8,128)(2,1)S(1)}, u32[]{:S(2)}, u32[]{:S(2)}) %all-to-all-start.1) | async-done | bytes 1572896 | tf_op jit(solution)/shard_map/all_to_all | solution.py:321
  96.1 13.4 %hidden.1 = (bf16[1280,512]{1,0:T(8,128)(2,1)S(1)}, f32[2,256,256]{2,1,0:T(8,128)S(1)}, f32[1,128]{1,0:T(1,128)S(1)}) custom-call(f32[2]{0:T(128)S(1)} %convert_bitcast_fusion.lev_ref, bf16[8,16,48,128]{3,2,1,0:T(8,128)(2,1)S(1)} %all-to-all-done.1.in_ref), custom_call_target="tpu_custom_call" | custom-call | tf_op jit(solution)/shard_map/hidden/pallas_call | solution.py:324
  109.5 11.1 %all-gather.2.cloned.1.call-done.x_ref = bf16[1280,4096]{1,0:T(8,128)(2,1)} async-done(((bf16[80,4096]{1,0:T(8,128)(2,1)}), bf16[1280,4096]{1,0:T(8,128)(2,1)}) %all-gather.2.cloned.1.call-update) | async-done | bytes 10485776 | tf_op jit(solution)/shard_map/all_gather | solution.py:319
  120.6 43.5 %solve.1 = (f32[16,256,512]{2,1,0:T(8,128)}, f32[8,128]{1,0:T(8,128)S(1)}) custom-call(f32[16]{0:T(128)S(1)} %convert_bitcast_fusion.1.lev_ref, f32[1,128]{1,0:T(1,128)S(1)} %get-tuple-element.18.count_ref, bf16[1280,4096]{1,0:T(8,128)(2,1)} %all-gather.2.cloned.1.call-done.x_ref, bf16[1280,512]{1,0:T(8,128)(2,1)S(1)} %get-tuple-element.27.h_ref, ...), custom_call_target="tpu_custom_call" | custom-call | tf_op jit(solution)/shard_map/solve/pallas_call | solution.py:339
  164.2 17.4 %all_to_all.19 = f32[128,1,128]{2,1,0:T(1,128)S(1)} all-to-all(f32[128,1,128]{2,1,0:T(1,128)S(1)} %broadcast_in_dim.4), channel_id=1, replica_groups=mesh['expert'=8,'shard'=16] {'expert','shard'}, dimensions={0} | all-to-all | bytes 131072 | tf_op jit(solution)/shard_map/all_to_all | solution.py:358
  181.6 6.2 %scale.1 = bf16[4096,512]{1,0:T(8,128)(2,1)} custom-call(f32[128,128]{1,0:T(8,128)S(1)} %bitcast.15, f32[4096,512]{1,0:T(8,128)} %bitcast.16), custom_call_target="tpu_custom_call" | custom-call | tf_op jit(solution)/shard_map/scale/pallas_call | solution.py:362
  (13 shorter events, 0.1 us)
Async XLA Ops:
  6.5 114.1 %all-gather.2.cloned.1.call-start = ((), (), s32[]{:S(2)}) async-start(), calls=%async_computation.3 | async-start | bytes 11141120 | tf_op jit(solution)/shard_map/all_gather | solution.py:319
  8.1 1.0 copy-start
  9.1 16.4 %copy-start.1 = (bf16[32,2,8192]{2,1,0:T(2,128)(2,1)S(1)}, bf16[32,2,8192]{2,1,0:T(2,128)(2,1)}, u32[]{:S(2)}) copy-start(bf16[32,2,8192]{2,1,0:T(2,128)(2,1)} %param.6) | copy-start | bytes 3145732
  9.6 7.8 %collective-permute-start = (bf16[40,1024]{1,0:T(8,128)(2,1)S(1)}, bf16[40,1024]{1,0:T(8,128)(2,1)S(1)}, u32[]{:S(2)}, u32[]{:S(2)}) collective-permute-start(bf16[40,1024]{1,0:T(8,128)(2,1)S(1)} %get-tuple-element.20), channel_id=1, source_target_pairs={{0,16},{16,32},{32,48},{48,64},{64,80},{80,96},{96,112},{112,0},{1... | collective-permute-start | bytes 245768 | tf_op jit(solution)/shard_map/ppermute | solution.py:293
  12.2 6.0 %collective-permute-start.1 = (bf16[40,1024]{1,0:T(8,128)(2,1)S(1)}, bf16[40,1024]{1,0:T(8,128)(2,1)S(1)}, u32[]{:S(2)}, u32[]{:S(2)}) collective-permute-start(bf16[40,1024]{1,0:T(8,128)(2,1)S(1)} %get-tuple-element.21), channel_id=1, source_target_pairs={{0,32},{16,48},{32,64},{48,80},{64,96},{80,112},{96,0},{112,16},{1... | collective-permute-start | bytes 245768 | tf_op jit(solution)/shard_map/ppermute | solution.py:293
  13.4 6.4 %collective-permute-start.2 = (bf16[40,1024]{1,0:T(8,128)(2,1)S(1)}, bf16[40,1024]{1,0:T(8,128)(2,1)S(1)}, u32[]{:S(2)}, u32[]{:S(2)}) collective-permute-start(bf16[40,1024]{1,0:T(8,128)(2,1)S(1)} %get-tuple-element.22), channel_id=1, source_target_pairs={{0,48},{16,64},{32,80},{48,96},{64,112},{80,0},{96,16},{112,32},{1... | collective-permute-start | bytes 245768 | tf_op jit(solution)/shard_map/ppermute | solution.py:293
  15.0 7.0 %collective-permute-start.3 = (bf16[40,1024]{1,0:T(8,128)(2,1)S(1)}, bf16[40,1024]{1,0:T(8,128)(2,1)S(1)}, u32[]{:S(2)}, u32[]{:S(2)}) collective-permute-start(bf16[40,1024]{1,0:T(8,128)(2,1)S(1)} %get-tuple-element.23), channel_id=1, source_target_pairs={{0,64},{16,80},{32,96},{48,112},{64,0},{80,16},{96,32},{112,48},{1... | collective-permute-start | bytes 245768 | tf_op jit(solution)/shard_map/ppermute | solution.py:293
  15.5 7.1 %collective-permute-start.4 = (bf16[40,1024]{1,0:T(8,128)(2,1)S(1)}, bf16[40,1024]{1,0:T(8,128)(2,1)S(1)}, u32[]{:S(2)}, u32[]{:S(2)}) collective-permute-start(bf16[40,1024]{1,0:T(8,128)(2,1)S(1)} %get-tuple-element.24), channel_id=1, source_target_pairs={{0,80},{16,96},{32,112},{48,0},{64,16},{80,32},{96,48},{112,64},{1... | collective-permute-start | bytes 245768 | tf_op jit(solution)/shard_map/ppermute | solution.py:293
  17.4 5.4 %collective-permute-start.5 = (bf16[40,1024]{1,0:T(8,128)(2,1)S(1)}, bf16[40,1024]{1,0:T(8,128)(2,1)S(1)}, u32[]{:S(2)}, u32[]{:S(2)}) collective-permute-start(bf16[40,1024]{1,0:T(8,128)(2,1)S(1)} %get-tuple-element.25), channel_id=1, source_target_pairs={{0,96},{16,112},{32,0},{48,16},{64,32},{80,48},{96,64},{112,80},{1... | collective-permute-start | bytes 245768 | tf_op jit(solution)/shard_map/ppermute | solution.py:293
  18.1 5.7 %collective-permute-start.6 = (bf16[40,1024]{1,0:T(8,128)(2,1)S(1)}, bf16[40,1024]{1,0:T(8,128)(2,1)S(1)}, u32[]{:S(2)}, u32[]{:S(2)}) collective-permute-start(bf16[40,1024]{1,0:T(8,128)(2,1)S(1)} %get-tuple-element.26), channel_id=1, source_target_pairs={{0,112},{16,0},{32,16},{48,32},{64,48},{80,64},{96,80},{112,96},{1... | collective-permute-start | bytes 245768 | tf_op jit(solution)/shard_map/ppermute | solution.py:293
  70.1 5.4 %copy-start.2 = (s32[1,16]{1,0:T(1,128)S(1)}, s32[1,16]{1,0:T(1,128)}, u32[]{:S(2)}) copy-start(s32[1,16]{1,0:T(1,128)} %param.8) | copy-start | bytes 196
  70.1 5.4 %copy-start.3 = (s32[1,2]{1,0:T(1,128)S(1)}, s32[1,2]{1,0:T(1,128)}, u32[]{:S(2)}) copy-start(s32[1,2]{1,0:T(1,128)} %param.9) | copy-start | bytes 28
  70.1 26.0 %all-to-all-start.1 = ((bf16[8,16,48,128]{3,2,1,0:T(8,128)(2,1)}), bf16[8,16,48,128]{3,2,1,0:T(8,128)(2,1)S(1)}, u32[]{:S(2)}, u32[]{:S(2)}) async-start(bf16[8,16,48,128]{3,2,1,0:T(8,128)(2,1)} %bitcast.14), calls=%async_computation.1 | async-start | bytes 3145728 | tf_op jit(solution)/shard_map/all_to_all | solution.py:321
Sparse Core Ops, SparseCore 0:
  25.5 95.0 all-gather.1

commit v2 on v1

--- a/solution.py
+++ b/solution.py
@@ -217,18 +217,19 @@
     s_ref[...] = -m_ref[...]
 
 
-def solve_kernel(lev_ref, count_ref, x_ref, h_ref, s_ref, out_hbm, sum_ref, m_ref, g_ref, out_sem):
+def solve_kernel(lev_ref, count_ref, x_ref, h_ref, s_ref, out_hbm, sum_ref, both_ref, m_ref, g_ref,
+                 out_sem):
     blocks, _, width = g_ref.shape
     cuts = [slice(c * BLK, (c + 1) * BLK) for c in range(width // BLK)]
 
     def store(b):
         return pltpu.make_async_copy(g_ref.at[b], out_hbm.at[b], out_sem.at[b])
 
+    both_ref[:, BLK:] = h_ref[...]
     for b in range(blocks):
         x = x_ref[:, b * BLK : (b + 1) * BLK]
-        both = lax.dot_general(
-            x, jnp.concatenate([x, h_ref[...]], 1), TN, preferred_element_type=F32
-        )
+        both_ref[:, :BLK] = x
+        both = lax.dot_general(x, both_ref[...], TN, preferred_element_type=F32)
         set_block(m_ref, b, both[:, :BLK], count_ref[:, :1], lev_ref[b])
         g_ref[b] = both[:, BLK:]
     invert_all(m_ref, blocks)
@@ -346,6 +347,7 @@
         in_specs=[sm, vm, vm, vm, vm],
         out_specs=(hbm, vm),
         scratch_shapes=[
+            pltpu.VMEM((shards * live, BLK + ff_dev), BF),
             pltpu.VMEM((blocks, BLK, BLK), F32),
             pltpu.VMEM((blocks, BLK, ff_dev), F32),
             pltpu.SemaphoreType.DMA((blocks,)),

time: 199 us -> 199 us (level)
  no operation moved by 1% of the time
where the time goes in v2:
time: 199 us; the launch traced here: 195 us
  Pallas kernels  67.2 us (34%)
  blocking collectives  58.1 us (29%)
  waiting for transfers between devices  35.4 us (18%)
  starting transfers between devices  15.9 us (8%)
  between operations  13.9 us (7%)
  local copies, waits for them, and re-layouts  4.38 us (2%)
    pallas_call x1, Pallas kernels, local(): call(solve_kernel, mib=44, out_shape=(pltpu.HBM((blocks, BLK, ff_dev), F3...  43.3 us
    all_to_all x1, blocking collectives, local(): received = lax.all_to_all(payload, 'shard', 0, 0, tiled=True)  40.7 us
    all_to_all x1, waiting for transfers between devices, local(): lax.all_to_all(received.transpose(1, 0, 2, 3), 'expert', 0, 0, tiled=True)  20.2 us
    all_to_all x1, blocking collectives, local(): lax.all_to_all(jnp.broadcast_to(norm, (devices, 128)), ('expert', 'shard'...  17.4 us
    pallas_call x1, Pallas kernels, local(): call(functools.partial(hidden_kernel, cap, ng), out_shape=[jax.ShapeDtype...  13.4 us
    all_gather x1, waiting for transfers between devices, local(): rows_x = lax.all_gather(x_group, 'shard', axis=0, tiled=True)  11.1 us
    ppermute x7, starting transfers between devices, local(): lax.ppermute(x_send[k], 'expert', [(e, (e + k) % groups) for e in range(g...  10.2 us
    pallas_call x1, Pallas kernels, local(): call(functools.partial(scale_kernel, float(groups * width * ff)), out_sha...  6.24 us
  transfers between devices with their start and end apart: 9, of which 6 were waited for; matrix products, arithmetic and copies ran while one was open for 1% of the time, Pallas kernels for 8%

profile of v2, /device:TPU:1, one launch (start us, length us, event | category | flops | bytes accessed | tf_op | source)
XLA Modules:
  0.0 195.0 jit_solution(2929262862215726780)
XLA Ops:
  6.5 0.8 slice_bitcast_fusion
  7.3 0.8 copy.16
  8.1 0.1 reshape.28.col_ref
  8.1 0.9 copy-done
  9.1 0.5 send_x.1
  9.6 2.6 %collective-permute-start = (bf16[40,1024]{1,0:T(8,128)(2,1)S(1)}, bf16[40,1024]{1,0:T(8,128)(2,1)S(1)}, u32[]{:S(2)}, u32[]{:S(2)}) collective-permute-start(bf16[40,1024]{1,0:T(8,128)(2,1)S(1)} %get-tuple-element.20), channel_id=1, source_target_pairs={{0,16},{16,32},{32,48},{48,64},{64,80},{80,96},{96,112},{112,0},{1... | collective-permute-start | bytes 245768 | tf_op jit(solution)/shard_map/ppermute | solution.py:294
  12.2 1.2 collective-permute-start.1
  13.4 1.6 collective-permute-start.2
  15.0 0.5 collective-permute-start.3
  15.5 1.9 collective-permute-start.4
  17.4 0.0 collective-permute-done.refs_1_
  17.4 0.7 collective-permute-start.5
  18.1 1.7 collective-permute-start.6
  19.8 0.0 collective-permute-done.2.refs_3_
  19.8 2.2 %collective-permute-done.3.refs_4_ = bf16[40,1024]{1,0:T(8,128)(2,1)S(1)} collective-permute-done((bf16[40,1024]{1,0:T(8,128)(2,1)S(1)}, bf16[40,1024]{1,0:T(8,128)(2,1)S(1)}, u32[]{:S(2)}, u32[]{:S(2)}) %collective-permute-start.3) | collective-permute-done | bytes 81952 | tf_op jit(solution)/shard_map/ppermute | solution.py:294
  22.0 0.6 collective-permute-done.4.refs_5_
  22.6 0.2 collective-permute-done.5.refs_6_
  22.8 1.1 collective-permute-done.6.refs_7_
  23.8 1.5 take_x.1
  25.4 0.0 all-gather.2.cloned.1.call-update
  25.4 0.1 reshape.24.row_ref
  25.5 0.4 reshape.25.g_ref
  26.0 2.3 %payload.1 = bf16[16,8,48,128]{3,2,1,0:T(8,128)(2,1)S(1)} custom-call(s32[64,1]{1,0:T(8,128)S(1)} %reshape.28.col_ref, s32[1,64]{1,0:T(1,128)S(1)} %reshape.24.row_ref, bf16[64,8192]{1,0:T(8,128)(2,1)S(1)} %reshape.25.g_ref), custom_call_target="tpu_custom_call" | custom-call | tf_op jit(solution)/shard_map/payload/pallas_call | solution.py:297
  28.2 40.7 %all_to_all.18 = bf16[16,8,48,128]{3,2,1,0:T(8,128)(2,1)S(1)} all-to-all(bf16[16,8,48,128]{3,2,1,0:T(8,128)(2,1)S(1)} %payload.1), channel_id=1, replica_groups=mesh['expert'=8,'shard'=16] {'shard'}, dimensions={0} | all-to-all | bytes 3145728 | tf_op jit(solution)/shard_map/all_to_all | solution.py:313
  68.9 1.2 copy.22
  70.1 5.7 %all-to-all-start.1 = ((bf16[8,16,48,128]{3,2,1,0:T(8,128)(2,1)}), bf16[8,16,48,128]{3,2,1,0:T(8,128)(2,1)S(1)}, u32[]{:S(2)}, u32[]{:S(2)}) async-start(bf16[8,16,48,128]{3,2,1,0:T(8,128)(2,1)} %bitcast.14), calls=%async_computation.1 | async-start | bytes 3145728 | tf_op jit(solution)/shard_map/all_to_all | solution.py:322
  75.9 20.2 %all-to-all-done.1.in_ref = bf16[8,16,48,128]{3,2,1,0:T(8,128)(2,1)S(1)} async-done(((bf16[8,16,48,128]{3,2,1,0:T(8,128)(2,1)}), bf16[8,16,48,128]{3,2,1,0:T(8,128)(2,1)S(1)}, u32[]{:S(2)}, u32[]{:S(2)}) %all-to-all-start.1) | async-done | bytes 1572896 | tf_op jit(solution)/shard_map/all_to_all | solution.py:322
  96.1 13.4 %hidden.1 = (bf16[1280,512]{1,0:T(8,128)(2,1)S(1)}, f32[2,256,256]{2,1,0:T(8,128)S(1)}, f32[1,128]{1,0:T(1,128)S(1)}) custom-call(f32[2]{0:T(128)S(1)} %convert_bitcast_fusion.lev_ref, bf16[8,16,48,128]{3,2,1,0:T(8,128)(2,1)S(1)} %all-to-all-done.1.in_ref), custom_call_target="tpu_custom_call" | custom-call | tf_op jit(solution)/shard_map/hidden/pallas_call | solution.py:325
  109.5 11.1 %all-gather.2.cloned.1.call-done.x_ref = bf16[1280,4096]{1,0:T(8,128)(2,1)} async-done(((bf16[80,4096]{1,0:T(8,128)(2,1)}), bf16[1280,4096]{1,0:T(8,128)(2,1)}) %all-gather.2.cloned.1.call-update) | async-done | bytes 10485776 | tf_op jit(solution)/shard_map/all_gather | solution.py:320
  120.6 43.3 %solve.1 = (f32[16,256,512]{2,1,0:T(8,128)}, f32[8,128]{1,0:T(8,128)S(1)}) custom-call(f32[16]{0:T(128)S(1)} %convert_bitcast_fusion.1.lev_ref, f32[1,128]{1,0:T(1,128)S(1)} %get-tuple-element.18.count_ref, bf16[1280,4096]{1,0:T(8,128)(2,1)} %all-gather.2.cloned.1.call-done.x_ref, bf16[1280,512]{1,0:T(8,128)(2,1)S(1)} %get-tuple-element.27.h_ref, ...), custom_call_target="tpu_custom_call" | custom-call | tf_op jit(solution)/shard_map/solve/pallas_call | solution.py:340
  164.0 17.4 %all_to_all.19 = f32[128,1,128]{2,1,0:T(1,128)S(1)} all-to-all(f32[128,1,128]{2,1,0:T(1,128)S(1)} %broadcast_in_dim.4), channel_id=1, replica_groups=mesh['expert'=8,'shard'=16] {'expert','shard'}, dimensions={0} | all-to-all | bytes 131072 | tf_op jit(solution)/shard_map/all_to_all | solution.py:360
  181.4 6.2 %scale.1 = bf16[4096,512]{1,0:T(8,128)(2,1)} custom-call(f32[128,128]{1,0:T(8,128)S(1)} %bitcast.15, f32[4096,512]{1,0:T(8,128)} %bitcast.16), custom_call_target="tpu_custom_call" | custom-call | tf_op jit(solution)/shard_map/scale/pallas_call | solution.py:364
  (13 shorter events, 0.1 us)
Async XLA Ops:
  6.5 114.1 %all-gather.2.cloned.1.call-start = ((), (), s32[]{:S(2)}) async-start(), calls=%async_computation.3 | async-start | bytes 11141120 | tf_op jit(solution)/shard_map/all_gather | solution.py:320
  8.1 1.0 copy-start
  9.1 16.4 %copy-start.1 = (bf16[32,2,8192]{2,1,0:T(2,128)(2,1)S(1)}, bf16[32,2,8192]{2,1,0:T(2,128)(2,1)}, u32[]{:S(2)}) copy-start(bf16[32,2,8192]{2,1,0:T(2,128)(2,1)} %param.6) | copy-start | bytes 3145732
  9.6 7.8 %collective-permute-start = (bf16[40,1024]{1,0:T(8,128)(2,1)S(1)}, bf16[40,1024]{1,0:T(8,128)(2,1)S(1)}, u32[]{:S(2)}, u32[]{:S(2)}) collective-permute-start(bf16[40,1024]{1,0:T(8,128)(2,1)S(1)} %get-tuple-element.20), channel_id=1, source_target_pairs={{0,16},{16,32},{32,48},{48,64},{64,80},{80,96},{96,112},{112,0},{1... | collective-permute-start | bytes 245768 | tf_op jit(solution)/shard_map/ppermute | solution.py:294
  12.2 5.9 %collective-permute-start.1 = (bf16[40,1024]{1,0:T(8,128)(2,1)S(1)}, bf16[40,1024]{1,0:T(8,128)(2,1)S(1)}, u32[]{:S(2)}, u32[]{:S(2)}) collective-permute-start(bf16[40,1024]{1,0:T(8,128)(2,1)S(1)} %get-tuple-element.21), channel_id=1, source_target_pairs={{0,32},{16,48},{32,64},{48,80},{64,96},{80,112},{96,0},{112,16},{1... | collective-permute-start | bytes 245768 | tf_op jit(solution)/shard_map/ppermute | solution.py:294
  13.4 6.4 %collective-permute-start.2 = (bf16[40,1024]{1,0:T(8,128)(2,1)S(1)}, bf16[40,1024]{1,0:T(8,128)(2,1)S(1)}, u32[]{:S(2)}, u32[]{:S(2)}) collective-permute-start(bf16[40,1024]{1,0:T(8,128)(2,1)S(1)} %get-tuple-element.22), channel_id=1, source_target_pairs={{0,48},{16,64},{32,80},{48,96},{64,112},{80,0},{96,16},{112,32},{1... | collective-permute-start | bytes 245768 | tf_op jit(solution)/shard_map/ppermute | solution.py:294
  15.0 7.0 %collective-permute-start.3 = (bf16[40,1024]{1,0:T(8,128)(2,1)S(1)}, bf16[40,1024]{1,0:T(8,128)(2,1)S(1)}, u32[]{:S(2)}, u32[]{:S(2)}) collective-permute-start(bf16[40,1024]{1,0:T(8,128)(2,1)S(1)} %get-tuple-element.23), channel_id=1, source_target_pairs={{0,64},{16,80},{32,96},{48,112},{64,0},{80,16},{96,32},{112,48},{1... | collective-permute-start | bytes 245768 | tf_op jit(solution)/shard_map/ppermute | solution.py:294
  15.5 7.1 %collective-permute-start.4 = (bf16[40,1024]{1,0:T(8,128)(2,1)S(1)}, bf16[40,1024]{1,0:T(8,128)(2,1)S(1)}, u32[]{:S(2)}, u32[]{:S(2)}) collective-permute-start(bf16[40,1024]{1,0:T(8,128)(2,1)S(1)} %get-tuple-element.24), channel_id=1, source_target_pairs={{0,80},{16,96},{32,112},{48,0},{64,16},{80,32},{96,48},{112,64},{1... | collective-permute-start | bytes 245768 | tf_op jit(solution)/shard_map/ppermute | solution.py:294
  17.4 5.4 %collective-permute-start.5 = (bf16[40,1024]{1,0:T(8,128)(2,1)S(1)}, bf16[40,1024]{1,0:T(8,128)(2,1)S(1)}, u32[]{:S(2)}, u32[]{:S(2)}) collective-permute-start(bf16[40,1024]{1,0:T(8,128)(2,1)S(1)} %get-tuple-element.25), channel_id=1, source_target_pairs={{0,96},{16,112},{32,0},{48,16},{64,32},{80,48},{96,64},{112,80},{1... | collective-permute-start | bytes 245768 | tf_op jit(solution)/shard_map/ppermute | solution.py:294
  18.1 5.7 %collective-permute-start.6 = (bf16[40,1024]{1,0:T(8,128)(2,1)S(1)}, bf16[40,1024]{1,0:T(8,128)(2,1)S(1)}, u32[]{:S(2)}, u32[]{:S(2)}) collective-permute-start(bf16[40,1024]{1,0:T(8,128)(2,1)S(1)} %get-tuple-element.26), channel_id=1, source_target_pairs={{0,112},{16,0},{32,16},{48,32},{64,48},{80,64},{96,80},{112,96},{1... | collective-permute-start | bytes 245768 | tf_op jit(solution)/shard_map/ppermute | solution.py:294
  70.1 5.7 %copy-start.2 = (s32[1,16]{1,0:T(1,128)S(1)}, s32[1,16]{1,0:T(1,128)}, u32[]{:S(2)}) copy-start(s32[1,16]{1,0:T(1,128)} %param.8) | copy-start | bytes 196
  70.1 5.7 %copy-start.3 = (s32[1,2]{1,0:T(1,128)S(1)}, s32[1,2]{1,0:T(1,128)}, u32[]{:S(2)}) copy-start(s32[1,2]{1,0:T(1,128)} %param.9) | copy-start | bytes 28
  70.1 26.0 %all-to-all-start.1 = ((bf16[8,16,48,128]{3,2,1,0:T(8,128)(2,1)}), bf16[8,16,48,128]{3,2,1,0:T(8,128)(2,1)S(1)}, u32[]{:S(2)}, u32[]{:S(2)}) async-start(bf16[8,16,48,128]{3,2,1,0:T(8,128)(2,1)} %bitcast.14), calls=%async_computation.1 | async-start | bytes 3145728 | tf_op jit(solution)/shard_map/all_to_all | solution.py:322
Sparse Core Ops, SparseCore 0:
  25.5 95.0 all-gather.1
